TPU v7x, 256 devices: a whole 4x4x8 slice. The times are simulated.
256 devices in a mesh: seq: 8 (over y, core), exp: 32 (over z, x).
Axes of the slice: x: 4, y: 4, z: 8, core: 2. Of those that a mesh axis runs over, the one named last changes fastest.
Arguments:
- query_rows: bfloat16 [4096, 4096], P('seq', 'exp'), may hold values from -6 to 6
- key_rows: bfloat16 [4096, 4096], P('seq', 'exp'), may hold values from -6 to 6
- value_rows: bfloat16 [4096, 4096], P('seq', 'exp'), may hold values from -6 to 6
- output_gate: bfloat16 [4096, 4096], P('seq', 'exp'), may hold values from -6 to 6
- log_decay: float32 [32, 4096], P('exp', 'seq'), may hold values from -0.8 to 0
- write_rate: float32 [32, 4096], P('exp', 'seq'), may hold values from 0.001 to 1
- doc_start: int32 [4096], P('seq'), may hold values from 0 to 1, as said below
- state_in: float32 [32, 128, 128], P('exp'), may hold values from -6 to 6
- head_gain: float32 [128], replicated, may hold values from 0.5 to 1.5
- out_weight: bfloat16 [4096, 2048], P('exp'), may hold values from -0.09375 to 0.09375
- residual: bfloat16 [4096, 2048], P(('seq', 'exp')), may hold values from -6 to 6
- post_gain: float32 [2048], replicated, may hold values from 0.5 to 1.5
- expert_ids: int32 [4096, 10], P(('seq', 'exp')), may hold values from 0 to 255, all different within a row; in each aligned block of 16 rows (0 to 15, 16 to 31, ...) at most 2 rows name the same one
- expert_scale: float32 [4096, 10], P(('seq', 'exp')), may hold values from 0.02 to 0.2
- w_gate_up: bfloat16 [256, 2048, 1024], P(('seq', 'exp')), may hold values from -0.125 to 0.125
- w_down: bfloat16 [256, 512, 2048], P(('seq', 'exp')), may hold values from -0.25 to 0.25
Outputs:
- layer_out: bfloat16 [4096, 2048], P(('seq', 'exp'))
Inputs may be any that keep to these rules, and one draw needn't show every extreme that they name: `doc_start`: one or two tokens after the first begin a new document. `expert_ids`: each token names 10 different experts; among the tokens of one device (aligned blocks of 512 // 32 rows) no expert is named more than 2 times, a bound that some block reaches.
All inputs are finite; a program needn't handle non-finite values.
Results may differ from a plain program's by a relative error of at most 0.014.
Values may be sent and summed in bfloat16 or wider, within the bound.
No kernel may reach another device: no remote copies, remote signals or barrier semaphores. Data moves between devices by JAX's collectives and lax.ppermute only.
A program may use at most 64 MiB of HBM per device.

v0:
```python
import jax
import jax.numpy as jnp
from jax import lax
from jax.sharding import PartitionSpec as P

DK = 128
DV = 128
FFE = 512
TOP = 10


def passed_along(array, axis, by):
    length = lax.axis_size(axis)
    pairs = [(i, i + by) for i in range(length) if 0 <= i + by < length]
    return lax.ppermute(array, axis, pairs)


def contract(form, left, right):
    return jnp.einsum(form, left, right, precision=lax.Precision.HIGHEST)


def by_blocks(rows, heads, block):
    length = rows.shape[0]
    width = rows.shape[1] // heads
    shaped = rows.astype(jnp.float32).reshape(length // block, block, heads, width)
    return shaped.transpose(2, 0, 1, 3)


def compose(earlier, later):
    return (
        contract("hkl,hlm->hkm", earlier[0], later[0]),
        contract("hvl,hlm->hvm", earlier[1], later[0]) + later[1],
    )


def local(
    query_rows,
    key_rows,
    value_rows,
    output_gate,
    log_decay,
    write_rate,
    doc_start,
    state_in,
    head_gain,
    out_weight,
    residual,
    post_gain,
    expert_ids,
    expert_scale,
    w_gate_up,
    w_down,
):
    length = query_rows.shape[0]
    heads = log_decay.shape[0]
    block = min(64, length)
    blocks = length // block
    query = by_blocks(query_rows, heads, block)
    key = by_blocks(key_rows, heads, block)
    key = key * lax.rsqrt(jnp.sum(key * key, axis=-1, keepdims=True) + 1e-06)
    value = by_blocks(value_rows, heads, block)
    decay_log = log_decay.reshape(heads, blocks, block)
    rate = write_rate.reshape(heads, blocks, block)
    resets = jnp.cumsum(doc_start.reshape(blocks, block), axis=-1)
    total_log = jnp.cumsum(decay_log, axis=-1)
    place = jnp.arange(block)
    within = place[:, None] >= place[None, :]
    strict = place[:, None] > place[None, :]
    same = (resets[:, :, None] == resets[:, None, :]) & within
    spread = total_log[..., :, None] - total_log[..., None, :]
    pair_decay = jnp.where(same, jnp.exp(jnp.where(same, spread, 0.0)), 0.0)
    start_decay = jnp.where(resets == 0, jnp.exp(total_log), 0.0)
    end_decay = jnp.where(resets == resets[:, -1:], jnp.exp(total_log[..., -1:] - total_log), 0.0)
    key_inner = contract("hbtk,hbsk->hbts", key, key)
    lower = jnp.where(strict, rate[..., :, None] * pair_decay * key_inner, 0.0)
    system = lower + jnp.eye(block, dtype=jnp.float32)
    right = jnp.concatenate(
        [rate[..., None] * value, (rate * start_decay)[..., None] * key], axis=-1
    )
    solved = lax.linalg.triangular_solve(
        system, right, left_side=True, lower=True, unit_diagonal=True
    )
    update = solved[..., :DV]
    erase = solved[..., DV:]
    tail_key = end_decay[..., None] * key
    identity = jnp.broadcast_to(jnp.eye(DK, dtype=jnp.float32), (heads, DK, DK))
    transfer = start_decay[..., -1, None, None] * identity[:, None] - contract(
        "hbtk,hbtl->hbkl", erase, tail_key
    )
    written = contract("hbtv,hbtk->hbvk", update, tail_key)
    scores = contract("hbtk,hbsk->hbts", query, key) * pair_decay

    def fold_block(carry, pair):
        return (compose(carry, pair), None)

    empty_state = jnp.zeros((heads, DV, DK), jnp.float32)
    moved_transfer = jnp.moveaxis(transfer, 1, 0)
    moved_written = jnp.moveaxis(written, 1, 0)
    (device_transfer, device_written), unused = lax.scan(
        fold_block, (identity, empty_state), (moved_transfer, moved_written)
    )
    first = lax.axis_index("seq") == 0

    def relay(turn, carry):
        sent = contract("hvk,hkl->hvl", carry, device_transfer) + device_written
        moved = passed_along(sent.astype(jnp.bfloat16), "seq", 1).astype(sent.dtype)
        return jnp.where(first, state_in, moved)

    start_state = lax.fori_loop(0, lax.axis_size("seq") - 1, relay, state_in)

    def run_block(state, pieces):
        query_now, update_now, erase_now, scores_now, start_now, transfer_now, written_now = pieces
        delta = update_now - contract("htk,hvk->htv", erase_now, state)
        output = start_now[..., None] * contract("htk,hvk->htv", query_now, state) + contract(
            "hts,hsv->htv", scores_now, delta
        )
        state = contract("hvk,hkl->hvl", state, transfer_now) + written_now
        return (state, output)

    pieces = (query, update, erase, scores, start_decay, transfer, written)
    final, outputs = lax.scan(
        run_block, start_state, tuple((jnp.moveaxis(piece, 1, 0) for piece in pieces))
    )
    head_out = jnp.moveaxis(outputs, 2, 1).reshape(length, heads, DV)
    gate = output_gate.astype(jnp.float32).reshape(length, heads, DV)
    scaled = head_out * lax.rsqrt(jnp.mean(head_out * head_out, axis=-1, keepdims=True) + 1e-06)
    gated = (
        (scaled * head_gain * jax.nn.silu(gate)).astype(jnp.bfloat16).reshape(length, heads * DV)
    )
    rows = residual.shape[0]
    width = residual.shape[1]
    attended = lax.psum_scatter(
        jnp.dot(gated, out_weight, preferred_element_type=jnp.float32).astype(jnp.bfloat16),
        "exp",
        scatter_dimension=0,
        tiled=True,
    ).astype(jnp.float32)
    stream = (residual.astype(jnp.float32) + attended).astype(jnp.bfloat16)
    wide = stream.astype(jnp.float32)
    normed = (
        wide * lax.rsqrt(jnp.mean(wide * wide, axis=-1, keepdims=True) + 1e-06) * post_gain
    ).astype(jnp.bfloat16)
    seq_count = lax.axis_size("seq")
    exp_count = lax.axis_size("exp")
    experts = seq_count * exp_count
    capacity = max(2, rows * TOP * 12 // (5 * experts))
    flat_ids = expert_ids.reshape(-1)
    hits = (flat_ids[:, None] == jnp.arange(experts, dtype=jnp.int32)[None, :]).astype(jnp.int32)
    rank = jnp.sum(jnp.cumsum(hits, axis=0) * hits, axis=1) - 1
    target = flat_ids * capacity + rank
    source_rows = jnp.repeat(normed, TOP, axis=0)
    outgoing = jnp.zeros((experts * capacity, width), jnp.bfloat16).at[target].set(source_rows)
    outgoing = outgoing.reshape(seq_count, exp_count, capacity, width)
    arrived = lax.all_to_all(
        lax.all_to_all(outgoing, "seq", split_axis=0, concat_axis=0, tiled=True),
        "exp",
        split_axis=1,
        concat_axis=1,
        tiled=True,
    )
    flat = arrived.reshape(-1, width)
    both = jnp.dot(flat, w_gate_up[0], preferred_element_type=jnp.float32)
    hidden = (jax.nn.silu(both[:, :FFE]) * both[:, FFE:]).astype(jnp.bfloat16)
    returned = lax.all_to_all(
        lax.all_to_all(
            jnp.dot(hidden, w_down[0], preferred_element_type=jnp.float32)
            .astype(jnp.bfloat16)
            .reshape(arrived.shape),
            "seq",
            split_axis=0,
            concat_axis=0,
            tiled=True,
        ),
        "exp",
        split_axis=1,
        concat_axis=1,
        tiled=True,
    )
    picked = returned.reshape(-1, width)[target].astype(jnp.float32).reshape(rows, TOP, width)
    moe = jnp.sum(expert_scale[..., None] * picked, axis=1)
    return (wide + moe).astype(jnp.bfloat16)


def solution(mesh):
    return jax.shard_map(
        local,
        mesh=mesh,
        in_specs=(
            P("seq", "exp"),
            P("seq", "exp"),
            P("seq", "exp"),
            P("seq", "exp"),
            P("exp", "seq"),
            P("exp", "seq"),
            P("seq"),
            P("exp", None, None),
            P(),
            P("exp", None),
            P(("seq", "exp"), None),
            P(),
            P(("seq", "exp"), None),
            P(("seq", "exp"), None),
            P(("seq", "exp"), None, None),
            P(("seq", "exp"), None, None),
        ),
        out_specs=P(("seq", "exp"), None),
        check_vma=False,
    )
```

profile of v0, /device:TPU:4, one launch (start us, length us, event | category | flops | bytes accessed | tf_op | source)
XLA Modules:
  0.0 599.0 jit_solution(11515922365121510422)
XLA Ops:
  14.5 39.3 %custom-call.3 = f32[1,8,1,64,64]{3,4,2,1,0:T(8,128)S(1)} custom-call(f32[1,8,1,64,64]{4,3,2,1,0:T(8,128)S(1)} %fusion.44), custom_call_target="InvertDiagBlocksLowerTriangular" | custom-call | tf_op jit(solution)/shard_map/triangular_solve | solution.py:80
  58.3 5.2 while.34
  65.7 42.1 %while.35 = (s32[]{:T(128)}, f32[1,128,128]{2,1,0:T(8,128)S(1)}, pred[]{:T(512)}, f32[1,128,128]{2,1,0:T(8,128)}, f32[1,128,128]{2,1,0:T(8,128)}, /*index=5*/f32[1,128,128]{2,1,0:T(8,128)}, s32[]{:T(128)}) while((s32[]{:T(128)}, f32[1,128,128]{2,1,0:T(8,128)S(1)}, pred[]{:T(512)}, f32[1,128,128]{2,1,0:T(8,128)}, f32[1,128,128]{2,1,0:T(8,128)}, ...), condition=%wide.region_6.7_spmd, body=%wide.region_5.6_spmd.sunk | while | flops 25231360 | bytes 524406 | solution.py:109
  66.8 1.7 collective-permute-start
  71.3 3.1 collective-permute-start
  77.2 3.6 collective-permute-start
  83.5 3.6 collective-permute-start
  89.9 3.6 collective-permute-start
  96.2 3.6 collective-permute-start
  102.6 3.6 collective-permute-start
  107.9 2.1 fusion.39
  110.9 24.3 %while.36 = (s32[]{:T(128)}, f32[1,128,128]{1,2,0:T(8,128)S(1)}, f32[8,1,64,128]{3,2,1,0:T(8,128)}, f32[8,1,128,128]{3,2,1,0:T(8,128)S(1)}, f32[8,1,128,128]{2,3...) while((s32[]{:T(128)}, f32[1,128,128]{1,2,0:T(8,128)S(1)}, ...), condition=%wide.region_8.9_spmd, body=%wide.region_7.8_spmd.sunk | while | flops 56664064 | bytes 823413 | solution.py:121
  137.7 3.1 convolution_convert_fusion
  141.7 222.1 %reduce-scatter.2.cloned.1.call-done = bf16[16,2048]{1,0:T(8,128)(2,1)} async-done(((bf16[512,2048]{1,0:T(8,128)(2,1)}), bf16[16,2048]{1,0:T(8,128)(2,1)}) %reduce-scatter.2.cloned.1.call-update) | async-done | bytes 65552 | tf_op jit(solution)/shard_map/reduce_scatter | solution.py:132
  366.9 3.8 scatter_custom_fusion
  370.7 4.4 reshape.481
  375.1 31.5 %all_to_all.20 = bf16[8,32,2,2048]{3,2,1,0:T(2,128)(2,1)S(1)} all-to-all(bf16[8,32,2,2048]{3,2,1,0:T(2,128)(2,1)} %reshape.481), channel_id=1, replica_groups=mesh['seq'=8,'exp'=32] {'seq'}, dimensions={0} | all-to-all | bytes 4194304 | tf_op jit(solution)/shard_map/all_to_all | solution.py:155
  406.6 2.3 copy.96
  408.9 57.9 %all_to_all.21 = bf16[8,32,2,2048]{3,2,0,1:T(2,128)(2,1)S(1)} all-to-all(bf16[8,32,2,2048]{3,2,0,1:T(2,128)(2,1)S(1)} %copy.96), channel_id=1, replica_groups=mesh['seq'=8,'exp'=32] {'exp'}, dimensions={1} | all-to-all | bytes 4194304 | tf_op jit(solution)/shard_map/all_to_all | solution.py:154
  466.8 3.1 copy.97
  469.9 4.1 reshape.482
  474.0 5.1 fusion.34
  479.2 2.6 convolution_convert_fusion.1
  481.8 4.4 reshape.483
  486.2 30.7 %all_to_all.22 = bf16[8,32,2,2048]{3,2,1,0:T(2,128)(2,1)S(1)} all-to-all(bf16[8,32,2,2048]{3,2,1,0:T(2,128)(2,1)} %reshape.483), channel_id=1, replica_groups=mesh['seq'=8,'exp'=32] {'seq'}, dimensions={0} | all-to-all | bytes 4194304 | tf_op jit(solution)/shard_map/all_to_all | solution.py:165
  517.0 3.6 copy.98
  520.5 5.6 all-to-all-start.3
  526.2 49.5 %all-to-all-done.3 = bf16[8,32,2,2048]{3,2,0,1:T(2,128)(2,1)} async-done(((bf16[8,32,2,2048]{3,2,0,1:T(2,128)(2,1)}), bf16[8,32,2,2048]{3,2,0,1:T(2,128)(2,1)}, u32[]{:S(2)}, u32[]{:S(2)}) %all-to-all-start.3) | async-done | bytes 2097184 | tf_op jit(solution)/shard_map/all_to_all | solution.py:164
  575.7 4.6 copy.99
  580.3 4.1 reshape.484
  584.4 3.5 gather_fusion
  589.5 2.1 multiply_reduce_fusion
  (185 shorter events, 72.0 us)
Async XLA Ops:
  6.5 472.6 %copy-start = (bf16[1,512,2048]{2,1,0:T(8,128)(2,1)S(1)}, bf16[1,512,2048]{2,1,0:T(8,128)(2,1)}, u32[]{:S(2)}) copy-start(bf16[1,512,2048]{2,1,0:T(8,128)(2,1)} %param.37) | copy-start | bytes 6291460
  6.5 47.6 %copy-start.3 = (bf16[512,128]{1,0:T(8,128)(2,1)S(1)}, bf16[512,128]{1,0:T(8,128)(2,1)}, u32[]{:S(2)}) copy-start(bf16[512,128]{1,0:T(8,128)(2,1)} %param.24) | copy-start | bytes 393220
  6.5 357.3 %reduce-scatter.2.cloned.1.call-start = ((), (), s32[]{:S(2)}) async-start(), calls=%async_computation.5 | async-start | bytes 2162688 | tf_op jit(solution)/shard_map/reduce_scatter | solution.py:132
  12.1 43.8 %copy-start.7 = (pred[64,64]{1,0:T(8,128)(4,1)}, pred[64,64]{1,0:T(8,128)(4,1)S(1)}, u32[]{:S(2)}) copy-start(pred[64,64]{1,0:T(8,128)(4,1)S(1)} %get-tuple-element.274) | copy-start | bytes 12292
  66.8 2.6 collective-permute-start
  71.3 4.0 collective-permute-start
  77.2 4.4 collective-permute-start
  83.5 4.4 collective-permute-start
  89.9 4.4 collective-permute-start
  96.2 4.4 collective-permute-start
  102.6 4.4 collective-permute-start
  110.9 25.5 %copy-start.8 = (f32[128]{0:T(128)S(1)}, f32[128]{0:T(128)}, u32[]{:S(2)}) copy-start(f32[128]{0:T(128)} %param.30) | copy-start | bytes 1540
  137.6 3.1 copy-start.4
  140.7 223.1 %copy-start.1 = (bf16[16,2048]{1,0:T(8,128)(2,1)S(1)}, bf16[16,2048]{1,0:T(8,128)(2,1)}, u32[]{:S(2)}) copy-start(bf16[16,2048]{1,0:T(8,128)(2,1)} %param.32) | copy-start | bytes 196612
  140.7 224.0 %copy-start.6 = (f32[2048]{0:T(1024)S(1)}, f32[2048]{0:T(1024)}, u32[]{:S(2)}) copy-start(f32[2048]{0:T(1024)} %param.33) | copy-start | bytes 24580
  520.5 55.2 %all-to-all-start.3 = ((bf16[8,32,2,2048]{3,2,0,1:T(2,128)(2,1)}), bf16[8,32,2,2048]{3,2,0,1:T(2,128)(2,1)}, u32[]{:S(2)}, u32[]{:S(2)}) async-start(bf16[8,32,2,2048]{3,2,0,1:T(2,128)(2,1)} %copy.98), calls=%async_computation.4 | async-start | bytes 4194304 | tf_op jit(solution)/shard_map/all_to_all | solution.py:164
  587.9 1.5 copy-start.5
  587.9 3.6 copy-start.2
Sparse Core Ops, SparseCore 0:
  140.9 222.8 reduce-scatter.1
where the time goes:
time: 602 us; the launch traced here: 599 us
  waiting for transfers between devices  278 us (46%)
  blocking collectives  120 us (20%)
  other arithmetic  59.3 us (10%)
  matrix products  52.6 us (9%)
  local copies, waits for them, and re-layouts  46.5 us (8%)
  starting transfers between devices  28.3 us (5%)
  between operations  13.7 us (2%)
    reduce_scatter x1, waiting for transfers between devices, local(): lax.psum_scatter(jnp.dot(gated, out_weight, preferred_element_type=jnp.fl...  222 us
    all_to_all x1, blocking collectives, local(): lax.all_to_all(lax.all_to_all(outgoing, 'seq', split_axis=0, concat_axis=...  57.9 us
    all_to_all x1, waiting for transfers between devices, local(): lax.all_to_all(lax.all_to_all(jnp.dot(hidden, w_down[0], preferred_elemen...  49.5 us
    dot_general x59, matrix products, contract(): return jnp.einsum(form, left, right, precision=lax.Precision.HIGHEST)  41.1 us
    another operation x4, other arithmetic, local(): lax.linalg.triangular_solve(system, right, left_side=True, lower=True, un...  39.4 us
    all_to_all x1, blocking collectives, local(): lax.all_to_all(outgoing, 'seq', split_axis=0, concat_axis=0, tiled=True)  31.5 us
    all_to_all x1, blocking collectives, local(): lax.all_to_all(jnp.dot(hidden, w_down[0], preferred_element_type=jnp.floa...  30.7 us
    ppermute x7, starting transfers between devices, passed_along(): return lax.ppermute(array, axis, pairs)  22.7 us
  transfers between devices with their start and end apart: 9, of which 9 were waited for; matrix products, arithmetic and copies ran while one was open for 0% of the time, Pallas kernels for 0%

commit v1 on v0

--- a/solution.py
+++ b/solution.py
@@ -1,3 +1,4 @@
+import functools
 import jax
 import jax.numpy as jnp
 from jax import lax
@@ -7,6 +8,16 @@
 DV = 128
 FFE = 512
 TOP = 10
+
+
+def get_circles(patch, along_axis):
+    return jnp.concatenate(
+        lax.all_to_all(jnp.stack(jnp.split(patch, lax.axis_size(along_axis), 1)), along_axis, 0, 0),
+        1,
+    )
+
+
+change_spot = functools.partial(get_circles, along_axis="exp")
 
 
 def passed_along(array, axis, by):
@@ -161,7 +172,7 @@
     flat = arrived.reshape(-1, width)
     both = jnp.dot(flat, w_gate_up[0], preferred_element_type=jnp.float32)
     hidden = (jax.nn.silu(both[:, :FFE]) * both[:, FFE:]).astype(jnp.bfloat16)
-    returned = lax.all_to_all(
+    returned = change_spot(
         lax.all_to_all(
             jnp.dot(hidden, w_down[0], preferred_element_type=jnp.float32)
             .astype(jnp.bfloat16)
@@ -170,11 +181,7 @@
             split_axis=0,
             concat_axis=0,
             tiled=True,
-        ),
-        "exp",
-        split_axis=1,
-        concat_axis=1,
-        tiled=True,
+        )
     )
     picked = returned.reshape(-1, width)[target].astype(jnp.float32).reshape(rows, TOP, width)
     moe = jnp.sum(expert_scale[..., None] * picked, axis=1)

time: 602 us -> 620 us (1.030)
  local copies, waits for them, and re-layouts: 46.5 us -> 64.2 us
    unnamed x21 -> x52, local copies, waits for them, and re-layouts: 1.46 us -> 22 us
    all_to_all x2 -> x0, local copies, waits for them, and re-layouts: 8.18 us -> none  [the longest x1 4.61 us: local(): lax.all_to_all(lax.all_to_all(jnp.dot(hidden, w_down[0], preferred_elemen...]
where the time goes in v1:
time: 620 us; the launch traced here: 617 us
  waiting for transfers between devices  278 us (45%)
  blocking collectives  120 us (19%)
  local copies, waits for them, and re-layouts  64.2 us (10%)
  other arithmetic  59.3 us (10%)
  matrix products  52.6 us (8%)
  starting transfers between devices  28.3 us (5%)
  between operations  13.8 us (2%)
    reduce_scatter x1, waiting for transfers between devices, local(): lax.psum_scatter(jnp.dot(gated, out_weight, preferred_element_type=jnp.fl...  222 us
    all_to_all x1, blocking collectives, local(): lax.all_to_all(lax.all_to_all(outgoing, 'seq', split_axis=0, concat_axis=...  57.9 us
    all_to_all x1, waiting for transfers between devices, get_circles(): lax.all_to_all(jnp.stack(jnp.split(patch, lax.axis_size(along_axis), 1)),...  49.5 us
    dot_general x59, matrix products, contract(): return jnp.einsum(form, left, right, precision=lax.Precision.HIGHEST)  41.1 us
    another operation x4, other arithmetic, local(): lax.linalg.triangular_solve(system, right, left_side=True, lower=True, un...  39.4 us
    all_to_all x1, blocking collectives, local(): lax.all_to_all(outgoing, 'seq', split_axis=0, concat_axis=0, tiled=True)  31.5 us
    all_to_all x1, blocking collectives, local(): lax.all_to_all(jnp.dot(hidden, w_down[0], preferred_element_type=jnp.floa...  30.7 us
    ppermute x7, starting transfers between devices, passed_along(): return lax.ppermute(array, axis, pairs)  22.7 us
  transfers between devices with their start and end apart: 9, of which 9 were waited for; matrix products, arithmetic and copies ran while one was open for 0% of the time, Pallas kernels for 0%

profile of v1, /device:TPU:4, one launch (start us, length us, event | category | flops | bytes accessed | tf_op | source)
XLA Modules:
  0.0 616.7 jit_solution(3993847111385925343)
XLA Ops:
  14.5 39.3 %custom-call.3 = f32[1,8,1,64,64]{3,4,2,1,0:T(8,128)S(1)} custom-call(f32[1,8,1,64,64]{4,3,2,1,0:T(8,128)S(1)} %fusion.44), custom_call_target="InvertDiagBlocksLowerTriangular" | custom-call | tf_op jit(solution)/shard_map/triangular_solve | solution.py:91
  58.3 5.2 while.34
  65.7 42.1 %while.35 = (s32[]{:T(128)}, f32[1,128,128]{2,1,0:T(8,128)S(1)}, pred[]{:T(512)}, f32[1,128,128]{2,1,0:T(8,128)}, f32[1,128,128]{2,1,0:T(8,128)}, /*index=5*/f32[1,128,128]{2,1,0:T(8,128)}, s32[]{:T(128)}) while((s32[]{:T(128)}, f32[1,128,128]{2,1,0:T(8,128)S(1)}, pred[]{:T(512)}, f32[1,128,128]{2,1,0:T(8,128)}, f32[1,128,128]{2,1,0:T(8,128)}, ...), condition=%wide.region_6.7_spmd, body=%wide.region_5.6_spmd.sunk | while | flops 25231360 | bytes 524406 | solution.py:120
  66.8 1.7 collective-permute-start
  71.3 3.1 collective-permute-start
  77.2 3.6 collective-permute-start
  83.5 3.6 collective-permute-start
  89.9 3.6 collective-permute-start
  96.2 3.6 collective-permute-start
  102.6 3.6 collective-permute-start
  107.9 2.1 fusion.39
  110.9 24.3 %while.36 = (s32[]{:T(128)}, f32[1,128,128]{1,2,0:T(8,128)S(1)}, f32[8,1,64,128]{3,2,1,0:T(8,128)}, f32[8,1,128,128]{3,2,1,0:T(8,128)S(1)}, f32[8,1,128,128]{2,3...) while((s32[]{:T(128)}, f32[1,128,128]{1,2,0:T(8,128)S(1)}, ...), condition=%wide.region_8.9_spmd, body=%wide.region_7.8_spmd.sunk | while | flops 56664064 | bytes 823413 | solution.py:132
  127.4 1.5 fusion.162
  137.7 3.1 convolution_convert_fusion
  141.7 222.1 %reduce-scatter.2.cloned.1.call-done = bf16[16,2048]{1,0:T(8,128)(2,1)} async-done(((bf16[512,2048]{1,0:T(8,128)(2,1)}), bf16[16,2048]{1,0:T(8,128)(2,1)}) %reduce-scatter.2.cloned.1.call-update) | async-done | bytes 65552 | tf_op jit(solution)/shard_map/reduce_scatter | solution.py:143
  366.9 3.8 scatter_custom_fusion
  370.7 4.4 reshape.481
  375.1 31.5 %all_to_all.20 = bf16[8,32,2,2048]{3,2,1,0:T(2,128)(2,1)S(1)} all-to-all(bf16[8,32,2,2048]{3,2,1,0:T(2,128)(2,1)} %reshape.481), channel_id=1, replica_groups=mesh['seq'=8,'exp'=32] {'seq'}, dimensions={0} | all-to-all | bytes 4194304 | tf_op jit(solution)/shard_map/all_to_all | solution.py:166
  406.6 2.3 copy.171
  408.9 57.9 %all_to_all.21 = bf16[8,32,2,2048]{3,2,0,1:T(2,128)(2,1)S(1)} all-to-all(bf16[8,32,2,2048]{3,2,0,1:T(2,128)(2,1)S(1)} %copy.171), channel_id=1, replica_groups=mesh['seq'=8,'exp'=32] {'exp'}, dimensions={1} | all-to-all | bytes 4194304 | tf_op jit(solution)/shard_map/all_to_all | solution.py:165
  466.8 3.1 copy.172
  469.9 4.1 reshape.482
  474.0 5.1 fusion.34
  479.2 2.6 convolution_convert_fusion.1
  481.8 4.4 reshape.483
  486.2 30.7 %all_to_all.22 = bf16[8,32,2,2048]{3,2,1,0:T(2,128)(2,1)S(1)} all-to-all(bf16[8,32,2,2048]{3,2,1,0:T(2,128)(2,1)} %reshape.483), channel_id=1, replica_groups=mesh['seq'=8,'exp'=32] {'seq'}, dimensions={0} | all-to-all | bytes 4194304 | tf_op jit(solution)/shard_map/all_to_all | solution.py:176
  538.2 5.6 all-to-all-start.3
  543.8 49.5 %all-to-all-done.3 = bf16[32,8,1,2,2048]{4,3,1,2,0:T(2,128)(2,1)} async-done(((bf16[32,8,1,2,2048]{4,3,1,2,0:T(2,128)(2,1)}), bf16[32,8,1,2,2048]{4,3,1,2,0:T(2,128)(2,1)}, u32[]{:S(2)}, u32[]{:S(2)}) %all-to-all-start.3) | async-done | bytes 2097184 | tf_op jit(solution)/shard_map/all_to_all | solution.py:15
  593.3 4.6 copy.204
  598.0 4.1 reshape_reshape.3
  602.1 3.5 gather_fusion
  607.2 2.1 multiply_reduce_fusion
  (216 shorter events, 91.7 us)
Async XLA Ops:
  6.5 472.6 %copy-start = (bf16[1,512,2048]{2,1,0:T(8,128)(2,1)S(1)}, bf16[1,512,2048]{2,1,0:T(8,128)(2,1)}, u32[]{:S(2)}) copy-start(bf16[1,512,2048]{2,1,0:T(8,128)(2,1)} %param.37) | copy-start | bytes 6291460
  6.5 47.6 %copy-start.3 = (bf16[512,128]{1,0:T(8,128)(2,1)S(1)}, bf16[512,128]{1,0:T(8,128)(2,1)}, u32[]{:S(2)}) copy-start(bf16[512,128]{1,0:T(8,128)(2,1)} %param.24) | copy-start | bytes 393220
  6.5 357.3 %reduce-scatter.2.cloned.1.call-start = ((), (), s32[]{:S(2)}) async-start(), calls=%async_computation.5 | async-start | bytes 2162688 | tf_op jit(solution)/shard_map/reduce_scatter | solution.py:143
  12.1 43.8 %copy-start.7 = (pred[64,64]{1,0:T(8,128)(4,1)}, pred[64,64]{1,0:T(8,128)(4,1)S(1)}, u32[]{:S(2)}) copy-start(pred[64,64]{1,0:T(8,128)(4,1)S(1)} %get-tuple-element.253) | copy-start | bytes 12292
  66.8 2.6 collective-permute-start
  71.3 4.0 collective-permute-start
  77.2 4.4 collective-permute-start
  83.5 4.4 collective-permute-start
  89.9 4.4 collective-permute-start
  96.2 4.4 collective-permute-start
  102.6 4.4 collective-permute-start
  110.9 25.5 %copy-start.8 = (f32[128]{0:T(128)S(1)}, f32[128]{0:T(128)}, u32[]{:S(2)}) copy-start(f32[128]{0:T(128)} %param.30) | copy-start | bytes 1540
  137.6 3.1 copy-start.4
  140.7 223.1 %copy-start.1 = (bf16[16,2048]{1,0:T(8,128)(2,1)S(1)}, bf16[16,2048]{1,0:T(8,128)(2,1)}, u32[]{:S(2)}) copy-start(bf16[16,2048]{1,0:T(8,128)(2,1)} %param.32) | copy-start | bytes 196612
  140.7 224.0 %copy-start.6 = (f32[2048]{0:T(1024)S(1)}, f32[2048]{0:T(1024)}, u32[]{:S(2)}) copy-start(f32[2048]{0:T(1024)} %param.33) | copy-start | bytes 24580
  538.2 55.2 %all-to-all-start.3 = ((bf16[32,8,1,2,2048]{4,3,1,2,0:T(2,128)(2,1)}), bf16[32,8,1,2,2048]{4,3,1,2,0:T(2,128)(2,1)}, u32[]{:S(2)}, u32[]{:S(2)}) async-start(bf16[32,8,1,2,2048]{4,3,1,2,0:T(2,128)(2,1)} %fusion.82), calls=%async_computation.4 | async-start | bytes 4194304 | tf_op jit(solution)/shard_map/all_to_all | solution.py:15
  605.6 1.5 copy-start.5
  605.6 3.6 copy-start.2
Sparse Core Ops, SparseCore 0:
  140.9 222.8 reduce-scatter.1
